TPU v7x, 256 devices: a whole 4x4x8 slice. The times are simulated.
256 devices in a mesh: dp: 4 (over x), seq: 64 (over z, y, core).
Axes of the slice: x: 4, y: 4, z: 8, core: 2. Of those that a mesh axis runs over, the one named last changes fastest.
Arguments:
- query_gate: bfloat16 [4, 8192, 4096], P('dp', 'seq'), may hold values from -6 to 6
- key_gate: bfloat16 [4, 8192, 4096], P('dp', 'seq'), may hold values from -6 to 6
- value_feat: bfloat16 [4, 8192, 4096], P('dp', 'seq'), may hold values from -6 to 6
- filters: bfloat16 [256, 128], replicated, may hold values from -0.5 to 0.5
- grad_out: bfloat16 [4, 8192, 4096], P('dp', 'seq'), may hold values from -6 to 6
- basis_prev: float32 [128, 16], replicated, may hold values from -6 to 6
Outputs:
- mixed_out: bfloat16 [4, 8192, 4096], P('dp', 'seq')
- grad_query: bfloat16 [4, 8192, 4096], P('dp', 'seq')
- grad_key: bfloat16 [4, 8192, 4096], P('dp', 'seq')
- grad_value: bfloat16 [4, 8192, 4096], P('dp', 'seq')
- low_rank_grad: float32 [256, 128], replicated
- basis_next: float32 [128, 16], replicated
All inputs are finite; a program needn't handle non-finite values.
Results may differ from a plain program's by a relative error of at most 0.0061.
Values may be sent and summed in bfloat16 or wider, within the bound.
No kernel may reach another device: no remote copies, remote signals or barrier semaphores. Data moves between devices by JAX's collectives and lax.ppermute only.
A program may use at most 192 MiB of HBM per device.

v0:
```python
import jax
import jax.numpy as jnp
from jax import lax
from jax.sharding import PartitionSpec as P


def shifted(block, axis, distance):
    devices = range(lax.axis_size(axis))
    route = [(i - distance, i) for i in devices if i - distance in devices]
    return lax.ppermute(block, axis, route)


def orthonormal(left):
    columns = []
    for index in range(left.shape[1]):
        column = left[:, index]
        if index > 0:
            basis = jnp.stack(columns, axis=1)
            coeffs = jnp.dot(basis.T, column, precision=lax.Precision.HIGHEST)
            column = column - jnp.dot(basis, coeffs, precision=lax.Precision.HIGHEST)
        columns.append(column / jnp.sqrt(jnp.sum(column * column) + 1e-06))
    return jnp.stack(columns, axis=1)


def banded(vec, rows):
    count, taps = vec.shape
    width = rows + taps - 1
    line = jnp.concatenate([vec, jnp.zeros((count, rows), vec.dtype)], axis=1)
    tiled = jnp.tile(line, (1, rows))[:, : rows * width]
    return tiled.reshape(count, rows, width)


def lag_sums(cross, taps):
    count, rows, width = cross.shape
    flat = cross.reshape(count, rows * width)[:, : (rows - 1) * 2 * taps]
    upper = flat.reshape(count, rows - 1, 2 * taps)[:, :, :taps].sum(axis=1)
    return upper + cross[:, rows - 1, rows - 1 : rows - 1 + taps]


def on_device(query_gate, key_gate, value_feat, filters, grad_out, basis_prev):
    gate_q = query_gate[0].astype(jnp.float32)
    gate_k = key_gate[0].astype(jnp.float32)
    feat_v = value_feat[0].astype(jnp.float32)
    cotan = grad_out[0].astype(jnp.float32)
    tok, channels = gate_q.shape
    groups, taps = filters.shape
    group_size = channels // groups
    width = tok + taps - 1
    product = (gate_k * feat_v).astype(jnp.bfloat16)
    grad_conv = (cotan * gate_q).astype(jnp.bfloat16)
    before = shifted(product[tok - (taps - 1) :], "seq", 1)
    after = shifted(grad_conv[: taps - 1], "seq", -1)
    prod_cm = jnp.concatenate([before, product], axis=0).T.reshape(groups, group_size, width)
    grad_cm = jnp.concatenate([grad_conv, after], axis=0).T.reshape(groups, group_size, width)
    block_groups = min(64, groups)
    conv_parts = []
    back_parts = []
    filter_parts = []
    for block in range(groups // block_groups):
        low = block * block_groups
        filt_blk = filters[low : low + block_groups]
        forward_tab = banded(filt_blk[:, ::-1], taps)
        backward_tab = banded(filt_blk, taps)
        prod_blk = prod_cm[low : low + block_groups]
        grad_blk = grad_cm[low : low + block_groups]
        conv_pos = jnp.einsum(
            "gcu,gsu->gcs", prod_blk, forward_tab, preferred_element_type=jnp.float32
        )
        back_pos = jnp.einsum(
            "gcu,gsu->gcs", grad_blk, backward_tab, preferred_element_type=jnp.float32
        )
        cross = jnp.einsum(
            "gcs,gcu->gsu", grad_blk[:, :, :taps], prod_blk, preferred_element_type=jnp.float32
        )
        lag_total = lag_sums(cross, taps)
        conv_parts.append(conv_pos)
        back_parts.append(back_pos)
        filter_parts.append(lag_total[:, ::-1])
    conv = jnp.concatenate(conv_parts, axis=0).reshape(channels, tok).T
    grad_product = jnp.concatenate(back_parts, axis=0).reshape(channels, tok).T
    local_grad = jnp.concatenate(filter_parts, axis=0)
    mixed_out = (gate_q * conv).astype(jnp.bfloat16)[None]
    grad_query = (cotan * conv).astype(jnp.bfloat16)[None]
    grad_key = (grad_product * feat_v).astype(jnp.bfloat16)[None]
    grad_value = (grad_product * gate_k).astype(jnp.bfloat16)[None]
    scale = (lax.axis_size("dp") * lax.axis_size("seq") * tok * group_size) ** (-0.5)
    seq_grad = lax.psum(local_grad, "seq")
    left = lax.psum(jnp.dot(seq_grad, basis_prev, precision=lax.Precision.HIGHEST), "dp")
    ortho = orthonormal(left)
    right = lax.psum(jnp.dot(seq_grad.T, ortho, precision=lax.Precision.HIGHEST), "dp")
    basis_next = right * scale
    low_rank_grad = jnp.dot(ortho, basis_next.T, precision=lax.Precision.HIGHEST)
    return (mixed_out, grad_query, grad_key, grad_value, low_rank_grad, basis_next)


def solution(mesh):
    return jax.shard_map(
        on_device,
        mesh=mesh,
        in_specs=(
            P("dp", "seq", None),
            P("dp", "seq", None),
            P("dp", "seq", None),
            P(),
            P("dp", "seq", None),
            P(),
        ),
        out_specs=(
            P("dp", "seq", None),
            P("dp", "seq", None),
            P("dp", "seq", None),
            P("dp", "seq", None),
            P(),
            P(),
        ),
        check_vma=False,
    )
```

profile of v0, /device:TPU:10, one launch (start us, length us, event | category | flops | bytes accessed | tf_op | source)
XLA Modules:
  0.0 581.4 jit_solution(8828656862283200973)
XLA Ops:
  16.9 16.3 %reshape.134 = bf16[64,128,255]{2,1,0:T(8,128)(2,1)} reshape(bf16[64,32640]{1,0:T(8,128)(2,1)} %slice.263) | data formatting | bytes 8355840 | tf_op jit(solution)/shard_map/reshape | solution.py:30
  38.3 15.8 %reshape.135 = bf16[64,128,255]{2,1,0:T(8,128)(2,1)} reshape(bf16[64,32640]{1,0:T(8,128)(2,1)} %slice.265) | data formatting | bytes 8355840 | tf_op jit(solution)/shard_map/reshape | solution.py:30
  59.2 16.0 %reshape.133 = bf16[64,128,255]{2,1,0:T(8,128)(2,1)} reshape(bf16[64,32640]{1,0:T(8,128)(2,1)} %slice.261) | data formatting | bytes 8355840 | tf_op jit(solution)/shard_map/reshape | solution.py:30
  80.3 15.8 %reshape.132 = bf16[64,128,255]{2,1,0:T(8,128)(2,1)} reshape(bf16[64,32640]{1,0:T(8,128)(2,1)} %slice.259) | data formatting | bytes 8355840 | tf_op jit(solution)/shard_map/reshape | solution.py:30
  97.4 3.6 fusion.64
  108.7 3.6 fusion.6
  120.4 15.8 %reshape.129 = bf16[64,128,255]{2,1,0:T(8,128)(2,1)} reshape(bf16[64,32640]{1,0:T(8,128)(2,1)} %slice.254) | data formatting | bytes 8355840 | tf_op jit(solution)/shard_map/reshape | solution.py:30
  141.3 15.8 %reshape.130 = bf16[64,128,255]{2,1,0:T(8,128)(2,1)} reshape(bf16[64,32640]{1,0:T(8,128)(2,1)} %slice.256) | data formatting | bytes 8355840 | tf_op jit(solution)/shard_map/reshape | solution.py:30
  162.2 16.0 %reshape.128 = bf16[64,128,255]{2,1,0:T(8,128)(2,1)} reshape(bf16[64,32640]{1,0:T(8,128)(2,1)} %slice.252) | data formatting | bytes 8355840 | tf_op jit(solution)/shard_map/reshape | solution.py:30
  183.3 15.8 %reshape.127 = bf16[64,128,255]{2,1,0:T(8,128)(2,1)} reshape(bf16[64,32640]{1,0:T(8,128)(2,1)} %slice.250) | data formatting | bytes 8355840 | tf_op jit(solution)/shard_map/reshape | solution.py:30
  202.4 3.2 copy-done.1
  205.8 9.5 %reshape.139 = f32[64,32640]{1,0:T(8,128)} reshape(f32[64,128,255]{2,1,0:T(8,128)} %copy-done.1) | data formatting | bytes 16711680 | tf_op jit(solution)/shard_map/reshape | solution.py:35
  216.8 3.2 copy-done.2
  220.1 9.3 %reshape.141 = f32[64,32640]{1,0:T(8,128)} reshape(f32[64,128,255]{2,1,0:T(8,128)} %copy-done.2) | data formatting | bytes 16711680 | tf_op jit(solution)/shard_map/reshape | solution.py:35
  230.9 3.2 copy-done.3
  234.3 9.3 %reshape.143 = f32[64,32640]{1,0:T(8,128)} reshape(f32[64,128,255]{2,1,0:T(8,128)} %copy-done.3) | data formatting | bytes 16711680 | tf_op jit(solution)/shard_map/reshape | solution.py:35
  245.1 3.2 copy-done.4
  248.5 9.3 %reshape.137 = f32[64,32640]{1,0:T(8,128)} reshape(f32[64,128,255]{2,1,0:T(8,128)} %copy-done.4) | data formatting | bytes 16711680 | tf_op jit(solution)/shard_map/reshape | solution.py:35
  257.8 3.5 fusion.58
  261.3 3.5 fusion.61
  270.7 7.1 %slice.271 = f32[64,32512]{1,0:T(8,128)} slice(f32[64,32640]{1,0:T(8,128)} %reshape.139), slice={[0:64], [0:32512]} | slice | bytes 16646144 | tf_op jit(solution)/shard_map/slice | solution.py:35
  277.8 7.7 %reshape.140 = f32[64,127,256]{2,1,0:T(8,128)} reshape(f32[64,32512]{1,0:T(8,128)} %slice.271) | data formatting | bytes 16646144 | tf_op jit(solution)/shard_map/reshape | solution.py:36
  288.2 7.1 %slice.275 = f32[64,32512]{1,0:T(8,128)} slice(f32[64,32640]{1,0:T(8,128)} %reshape.141), slice={[0:64], [0:32512]} | slice | bytes 16646144 | tf_op jit(solution)/shard_map/slice | solution.py:35
  295.3 7.4 %reshape.142 = f32[64,127,256]{2,1,0:T(8,128)} reshape(f32[64,32512]{1,0:T(8,128)} %slice.275) | data formatting | bytes 16646144 | tf_op jit(solution)/shard_map/reshape | solution.py:36
  305.4 7.1 %slice.279 = f32[64,32512]{1,0:T(8,128)} slice(f32[64,32640]{1,0:T(8,128)} %reshape.143), slice={[0:64], [0:32512]} | slice | bytes 16646144 | tf_op jit(solution)/shard_map/slice | solution.py:35
  312.5 7.4 %reshape.144 = f32[64,127,256]{2,1,0:T(8,128)} reshape(f32[64,32512]{1,0:T(8,128)} %slice.279) | data formatting | bytes 16646144 | tf_op jit(solution)/shard_map/reshape | solution.py:36
  322.7 7.1 %slice.267 = f32[64,32512]{1,0:T(8,128)} slice(f32[64,32640]{1,0:T(8,128)} %reshape.137), slice={[0:64], [0:32512]} | slice | bytes 16646144 | tf_op jit(solution)/shard_map/slice | solution.py:35
  329.8 7.4 %reshape.138 = f32[64,127,256]{2,1,0:T(8,128)} reshape(f32[64,32512]{1,0:T(8,128)} %slice.267) | data formatting | bytes 16646144 | tf_op jit(solution)/shard_map/reshape | solution.py:36
  340.8 3.0 fusion.9
  343.8 174.6 %all-reduce.10.cloned.1.call-done = f32[256,128]{1,0:T(8,128)} async-done(((f32[256,128]{1,0:T(8,128)}), f32[256,128]{1,0:T(8,128)}) %all-reduce.10.cloned.1.call-update) | async-done | bytes 131088 | tf_op jit(solution)/shard_map/psum | solution.py:87
  519.5 13.9 %psum.22 = f32[256,16]{0,1:T(8,128)S(1)} all-reduce(f32[256,16]{0,1:T(8,128)S(1)} %fusion.66), channel_id=1, replica_groups=mesh['dp'=4,'seq'=64] {'dp'}, use_global_device_ids=true, to_apply=%region_5.0 | all-reduce | flops 4096 | bytes 32768 | tf_op jit(solution)/shard_map/psum | solution.py:88
  561.9 11.3 %psum.23 = f32[128,16]{0,1:T(8,128)S(1)} all-reduce(f32[128,16]{0,1:T(8,128)S(1)} %fusion.78), channel_id=1, replica_groups=mesh['dp'=4,'seq'=64] {'dp'}, use_global_device_ids=true, to_apply=%region_22.0 | all-reduce | flops 2048 | bytes 16384 | tf_op jit(solution)/shard_map/psum | solution.py:90
  (200 shorter events, 102.1 us)
Async XLA Ops:
  7.2 511.2 %copy-start = (f32[128,16]{0,1:T(8,128)S(1)}, f32[128,16]{0,1:T(8,128)}, u32[]{:S(2)}) copy-start(f32[128,16]{0,1:T(8,128)} %param.11) | copy-start | bytes 24580
  7.2 511.2 %all-reduce.10.cloned.1.call-start = ((), (), s32[]{:S(2)}) async-start(), calls=%async_computation | async-start | bytes 262144 | tf_op jit(solution)/shard_map/psum | solution.py:87
  9.0 87.1 %collective-permute-start.1 = (bf16[127,4096]{1,0:T(8,128)(2,1)S(1)}, bf16[127,4096]{1,0:T(8,128)(2,1)S(1)}, u32[]{:S(2)}, u32[]{:S(2)}) collective-permute-start(bf16[127,4096]{1,0:T(8,128)(2,1)S(1)} %bitcast.286), channel_id=1, source_target_pairs={{1,0},{2,1},{3,2},{4,3},{5,4},{6,5},{7,6},{8,7},{9,8},{10,9},{11,1... | collective-permute-start | bytes 3121160 | tf_op jit(solution)/shard_map/ppermute | solution.py:10
  96.7 6.7 %copy-start.11 = (bf16[1024,255]{1,0:T(8,128)(2,1)}, bf16[1024,255]{1,0:T(8,128)(2,1)S(1)}, u32[]{:S(2)}) copy-start(bf16[1024,255]{1,0:T(8,128)(2,1)S(1)} %copy.30) | copy-start | bytes 1566724
  96.9 5.3 copy-start.13
  97.1 5.1 copy-start.15
  97.3 4.9 copy-start.17
  97.4 3.6 copy-start.7
  97.4 4.9 copy-start.8
  101.0 2.7 copy-start.9
  112.5 86.5 %collective-permute-start = (bf16[127,4096]{1,0:T(8,128)(2,1)S(1)}, bf16[127,4096]{1,0:T(8,128)(2,1)}, u32[]{:S(2)}, u32[]{:S(2)}) collective-permute-start(bf16[127,4096]{1,0:T(8,128)(2,1)S(1)} %slice.248), channel_id=1, source_target_pairs={{0,1},{1,2},{2,3},{3,4},{4,5},{5,6},{6,7},{7,8},{8,9},{9,10},{10,1... | collective-permute-start | bytes 3121160 | tf_op jit(solution)/shard_map/ppermute | solution.py:10
  199.1 2.0 copy-start.18
  202.4 3.2 copy-start.1
  205.8 9.7 %copy-start.16 = (bf16[1024,255]{1,0:T(8,128)(2,1)S(1)}, bf16[1024,255]{1,0:T(8,128)(2,1)}, u32[]{:S(2)}) copy-start(bf16[1024,255]{1,0:T(8,128)(2,1)} %copy-done.15) | copy-start | bytes 1566724
  216.8 3.2 copy-start.2
  220.1 9.5 %copy-start.14 = (bf16[1024,255]{1,0:T(8,128)(2,1)S(1)}, bf16[1024,255]{1,0:T(8,128)(2,1)}, u32[]{:S(2)}) copy-start(bf16[1024,255]{1,0:T(8,128)(2,1)} %copy-done.13) | copy-start | bytes 1566724
  230.9 3.2 copy-start.3
  234.3 9.5 %copy-start.12 = (bf16[1024,255]{1,0:T(8,128)(2,1)S(1)}, bf16[1024,255]{1,0:T(8,128)(2,1)}, u32[]{:S(2)}) copy-start(bf16[1024,255]{1,0:T(8,128)(2,1)} %copy-done.11) | copy-start | bytes 1566724
  245.1 3.2 copy-start.4
  257.8 7.1 %copy-start.5 = (bf16[64,128,255]{2,1,0:T(8,128)(2,1)S(1)}, bf16[64,128,255]{2,1,0:T(8,128)(2,1)}, u32[]{:S(2)}) copy-start(bf16[64,128,255]{2,1,0:T(8,128)(2,1)} %reshape.129) | copy-start | bytes 12533764
  261.3 4.8 copy-start.6
  337.2 3.5 copy-start.10
  573.2 1.1 copy-start.19
Sparse Core Ops, SparseCore 0:
  340.9 177.4 all-reduce.9
where the time goes:
time: 586 us; the launch traced here: 581 us
  local copies, waits for them, and re-layouts  286 us (49%)
  waiting for transfers between devices  175 us (30%)
  other arithmetic  36.3 us (6%)
  matrix products  28.7 us (5%)
  between operations  26.1 us (4%)
  blocking collectives  25.2 us (4%)
    psum x1, waiting for transfers between devices, on_device(): seq_grad = lax.psum(local_grad, 'seq')  175 us
    reshape x8, local copies, waits for them, and re-layouts, banded(): return tiled.reshape(count, rows, width)  127 us
    reshape x4, local copies, waits for them, and re-layouts, lag_sums(): flat = cross.reshape(count, rows * width)[:, :(rows - 1) * 2 * taps]  37.3 us
    unnamed x48, local copies, waits for them, and re-layouts  33.8 us
    reshape x4, local copies, waits for them, and re-layouts, lag_sums(): upper = flat.reshape(count, rows - 1, 2 * taps)[:, :, :taps].sum(axis=1)  30 us
    slice x4, local copies, waits for them, and re-layouts, lag_sums(): flat = cross.reshape(count, rows * width)[:, :(rows - 1) * 2 * taps]  28.4 us
    slice x8, local copies, waits for them, and re-layouts, banded(): tiled = jnp.tile(line, (1, rows))[:, :rows * width]  17.7 us
    psum x1, blocking collectives, on_device(): lax.psum(jnp.dot(seq_grad, basis_prev, precision=lax.Precision.HIGHEST),...  13.9 us
  transfers between devices with their start and end apart: 3, of which 1 were waited for; matrix products, arithmetic and copies ran while one was open for 30% of the time, Pallas kernels for 0%

commit v1 on v0

--- a/solution.py
+++ b/solution.py
@@ -2,6 +2,12 @@
 import jax.numpy as jnp
 from jax import lax
 from jax.sharding import PartitionSpec as P
+
+
+def summed_here(shard, mesh_axis):
+    parts = lax.all_gather(shard, mesh_axis, axis=0, tiled=False)
+    acc = parts.sum(axis=0)
+    return acc
 
 
 def shifted(block, axis, distance):
@@ -84,7 +90,7 @@
     grad_key = (grad_product * feat_v).astype(jnp.bfloat16)[None]
     grad_value = (grad_product * gate_k).astype(jnp.bfloat16)[None]
     scale = (lax.axis_size("dp") * lax.axis_size("seq") * tok * group_size) ** (-0.5)
-    seq_grad = lax.psum(local_grad, "seq")
+    seq_grad = summed_here(local_grad, "seq")
     left = lax.psum(jnp.dot(seq_grad, basis_prev, precision=lax.Precision.HIGHEST), "dp")
     ortho = orthonormal(left)
     right = lax.psum(jnp.dot(seq_grad.T, ortho, precision=lax.Precision.HIGHEST), "dp")

time: 586 us -> 433 us (0.74)
  the two profiles are of different devices: /device:TPU:10 before, /device:TPU:130 now
where the time goes in v1:
time: 433 us; the launch traced here: 429 us
  local copies, waits for them, and re-layouts  288 us (67%)
  other arithmetic  38.8 us (9%)
  matrix products  26.9 us (6%)
  between operations  26.1 us (6%)
  blocking collectives  25.3 us (6%)
  waiting for transfers between devices  17.5 us (4%)
  starting transfers between devices  6 us (1%)
    reshape x8, local copies, waits for them, and re-layouts, banded(): return tiled.reshape(count, rows, width)  128 us
    reshape x4, local copies, waits for them, and re-layouts, lag_sums(): flat = cross.reshape(count, rows * width)[:, :(rows - 1) * 2 * taps]  37.1 us
    unnamed x42, local copies, waits for them, and re-layouts  33.8 us
    reshape x4, local copies, waits for them, and re-layouts, lag_sums(): upper = flat.reshape(count, rows - 1, 2 * taps)[:, :, :taps].sum(axis=1)  30.1 us
    slice x4, local copies, waits for them, and re-layouts, lag_sums(): flat = cross.reshape(count, rows * width)[:, :(rows - 1) * 2 * taps]  28.4 us
    slice x8, local copies, waits for them, and re-layouts, banded(): tiled = jnp.tile(line, (1, rows))[:, :rows * width]  17.8 us
    ppermute x2, waiting for transfers between devices, shifted(): return lax.ppermute(block, axis, route)  17.5 us
    psum x1, blocking collectives, on_device(): lax.psum(jnp.dot(seq_grad, basis_prev, precision=lax.Precision.HIGHEST),...  14 us
  transfers between devices with their start and end apart: 3, of which 1 were waited for; matrix products, arithmetic and copies ran while one was open for 43% of the time, Pallas kernels for 0%

profile of v1, /device:TPU:130, one launch (start us, length us, event | category | flops | bytes accessed | tf_op | source)
XLA Modules:
  0.0 428.5 jit_solution(4786786200335548332)
XLA Ops:
  9.0 3.9 collective-permute-start.1
  18.9 16.3 %reshape.134 = bf16[64,128,255]{2,1,0:T(8,128)(2,1)} reshape(bf16[64,32640]{1,0:T(8,128)(2,1)} %slice.263) | data formatting | bytes 8355840 | tf_op jit(solution)/shard_map/reshape | solution.py:36
  40.3 15.8 %reshape.135 = bf16[64,128,255]{2,1,0:T(8,128)(2,1)} reshape(bf16[64,32640]{1,0:T(8,128)(2,1)} %slice.265) | data formatting | bytes 8355840 | tf_op jit(solution)/shard_map/reshape | solution.py:36
  61.2 16.0 %reshape.133 = bf16[64,128,255]{2,1,0:T(8,128)(2,1)} reshape(bf16[64,32640]{1,0:T(8,128)(2,1)} %slice.261) | data formatting | bytes 8355840 | tf_op jit(solution)/shard_map/reshape | solution.py:36
  82.2 15.8 %reshape.132 = bf16[64,128,255]{2,1,0:T(8,128)(2,1)} reshape(bf16[64,32640]{1,0:T(8,128)(2,1)} %slice.259) | data formatting | bytes 8355840 | tf_op jit(solution)/shard_map/reshape | solution.py:36
  99.3 3.6 fusion.64
  110.4 3.6 fusion.6
  116.3 17.5 %collective-permute-done = bf16[127,4096]{1,0:T(8,128)(2,1)S(1)} collective-permute-done((bf16[127,4096]{1,0:T(8,128)(2,1)S(1)}, bf16[127,4096]{1,0:T(8,128)(2,1)S(1)}, u32[]{:S(2)}, u32[]{:S(2)}) %collective-permute-start) | collective-permute-done | bytes 1040416 | tf_op jit(solution)/shard_map/ppermute | solution.py:16
  136.8 3.2 copy-done.1
  140.2 9.3 %reshape.139 = f32[64,32640]{1,0:T(8,128)} reshape(f32[64,128,255]{2,1,0:T(8,128)} %copy-done.1) | data formatting | bytes 16711680 | tf_op jit(solution)/shard_map/reshape | solution.py:41
  152.0 3.2 copy-done.2
  155.4 9.2 %reshape.141 = f32[64,32640]{1,0:T(8,128)} reshape(f32[64,128,255]{2,1,0:T(8,128)} %copy-done.2) | data formatting | bytes 16711680 | tf_op jit(solution)/shard_map/reshape | solution.py:41
  166.1 3.2 copy-done.3
  169.5 9.3 %reshape.143 = f32[64,32640]{1,0:T(8,128)} reshape(f32[64,128,255]{2,1,0:T(8,128)} %copy-done.3) | data formatting | bytes 16711680 | tf_op jit(solution)/shard_map/reshape | solution.py:41
  183.7 9.3 %reshape.137 = f32[64,32640]{1,0:T(8,128)} reshape(f32[64,128,255]{2,1,0:T(8,128)} %copy-done.4) | data formatting | bytes 16711680 | tf_op jit(solution)/shard_map/reshape | solution.py:41
  192.9 7.1 %slice.271 = f32[64,32512]{1,0:T(8,128)} slice(f32[64,32640]{1,0:T(8,128)} %reshape.139), slice={[0:64], [0:32512]} | slice | bytes 16646144 | tf_op jit(solution)/shard_map/slice | solution.py:41
  200.0 7.4 %reshape.140 = f32[64,127,256]{2,1,0:T(8,128)} reshape(f32[64,32512]{1,0:T(8,128)} %slice.271) | data formatting | bytes 16646144 | tf_op jit(solution)/shard_map/reshape | solution.py:42
  210.2 7.1 %slice.275 = f32[64,32512]{1,0:T(8,128)} slice(f32[64,32640]{1,0:T(8,128)} %reshape.141), slice={[0:64], [0:32512]} | slice | bytes 16646144 | tf_op jit(solution)/shard_map/slice | solution.py:41
  217.3 7.8 %reshape.142 = f32[64,127,256]{2,1,0:T(8,128)} reshape(f32[64,32512]{1,0:T(8,128)} %slice.275) | data formatting | bytes 16646144 | tf_op jit(solution)/shard_map/reshape | solution.py:42
  227.8 7.1 %slice.279 = f32[64,32512]{1,0:T(8,128)} slice(f32[64,32640]{1,0:T(8,128)} %reshape.143), slice={[0:64], [0:32512]} | slice | bytes 16646144 | tf_op jit(solution)/shard_map/slice | solution.py:41
  234.9 7.4 %reshape.144 = f32[64,127,256]{2,1,0:T(8,128)} reshape(f32[64,32512]{1,0:T(8,128)} %slice.279) | data formatting | bytes 16646144 | tf_op jit(solution)/shard_map/reshape | solution.py:42
  245.1 7.1 %slice.267 = f32[64,32512]{1,0:T(8,128)} slice(f32[64,32640]{1,0:T(8,128)} %reshape.137), slice={[0:64], [0:32512]} | slice | bytes 16646144 | tf_op jit(solution)/shard_map/slice | solution.py:41
  252.2 7.4 %reshape.138 = f32[64,127,256]{2,1,0:T(8,128)} reshape(f32[64,32512]{1,0:T(8,128)} %slice.267) | data formatting | bytes 16646144 | tf_op jit(solution)/shard_map/reshape | solution.py:42
  268.6 16.0 %reshape.129 = bf16[64,128,255]{2,1,0:T(8,128)(2,1)} reshape(bf16[64,32640]{1,0:T(8,128)(2,1)} %slice.254) | data formatting | bytes 8355840 | tf_op jit(solution)/shard_map/reshape | solution.py:36
  289.6 15.9 %reshape.130 = bf16[64,128,255]{2,1,0:T(8,128)(2,1)} reshape(bf16[64,32640]{1,0:T(8,128)(2,1)} %slice.256) | data formatting | bytes 8355840 | tf_op jit(solution)/shard_map/reshape | solution.py:36
  310.6 16.0 %reshape.128 = bf16[64,128,255]{2,1,0:T(8,128)(2,1)} reshape(bf16[64,32640]{1,0:T(8,128)(2,1)} %slice.252) | data formatting | bytes 8355840 | tf_op jit(solution)/shard_map/reshape | solution.py:36
  331.7 15.8 %reshape.127 = bf16[64,128,255]{2,1,0:T(8,128)(2,1)} reshape(bf16[64,32640]{1,0:T(8,128)(2,1)} %slice.250) | data formatting | bytes 8355840 | tf_op jit(solution)/shard_map/reshape | solution.py:36
  347.5 3.5 fusion.58
  351.0 3.5 fusion.61
  363.5 3.8 reduce_sum.193
  367.5 14.0 %psum.14 = f32[256,16]{0,1:T(8,128)S(1)} all-reduce(f32[256,16]{0,1:T(8,128)S(1)} %fusion.66), channel_id=1, replica_groups=mesh['dp'=4,'seq'=64] {'dp'}, use_global_device_ids=true, to_apply=%region_5.0 | all-reduce | flops 4096 | bytes 32768 | tf_op jit(solution)/shard_map/psum | solution.py:94
  409.1 11.3 %psum.15 = f32[128,16]{0,1:T(8,128)S(1)} all-reduce(f32[128,16]{0,1:T(8,128)S(1)} %fusion.78), channel_id=1, replica_groups=mesh['dp'=4,'seq'=64] {'dp'}, use_global_device_ids=true, to_apply=%region_22.0 | all-reduce | flops 2048 | bytes 16384 | tf_op jit(solution)/shard_map/psum | solution.py:96
  (195 shorter events, 104.9 us)
Async XLA Ops:
  7.2 360.2 %copy-start = (f32[128,16]{0,1:T(8,128)S(1)}, f32[128,16]{0,1:T(8,128)}, u32[]{:S(2)}) copy-start(f32[128,16]{0,1:T(8,128)} %param.11) | copy-start | bytes 24580
  7.2 356.4 %all-gather.3.cloned.1.call-start = ((), (), s32[]{:S(2)}) async-start(), calls=%async_computation | async-start | bytes 8519680 | tf_op jit(solution)/shard_map/all_gather | solution.py:8
  9.0 89.0 %collective-permute-start.1 = (bf16[127,4096]{1,0:T(8,128)(2,1)S(1)}, bf16[127,4096]{1,0:T(8,128)(2,1)S(1)}, u32[]{:S(2)}, u32[]{:S(2)}) collective-permute-start(bf16[127,4096]{1,0:T(8,128)(2,1)S(1)} %bitcast.288), channel_id=1, source_target_pairs={{1,0},{2,1},{3,2},{4,3},{5,4},{6,5},{7,6},{8,7},{9,8},{10,9},{11,1... | collective-permute-start | bytes 3121160 | tf_op jit(solution)/shard_map/ppermute | solution.py:16
  99.0 5.0 %copy-start.11 = (bf16[1024,255]{1,0:T(8,128)(2,1)}, bf16[1024,255]{1,0:T(8,128)(2,1)S(1)}, u32[]{:S(2)}) copy-start(bf16[1024,255]{1,0:T(8,128)(2,1)S(1)} %copy.32) | copy-start | bytes 1566724
  99.2 4.8 %copy-start.13 = (bf16[1024,255]{1,0:T(8,128)(2,1)}, bf16[1024,255]{1,0:T(8,128)(2,1)S(1)}, u32[]{:S(2)}) copy-start(bf16[1024,255]{1,0:T(8,128)(2,1)S(1)} %copy.31) | copy-start | bytes 1566724
  99.2 3.6 copy-start.5
  99.3 4.9 %copy-start.6 = (bf16[64,128,255]{2,1,0:T(8,128)(2,1)S(1)}, bf16[64,128,255]{2,1,0:T(8,128)(2,1)}, u32[]{:S(2)}) copy-start(bf16[64,128,255]{2,1,0:T(8,128)(2,1)} %reshape.133) | copy-start | bytes 12533764
  102.9 2.7 copy-start.8
  114.2 21.3 %copy-start.14 = (bf16[1024,255]{1,0:T(8,128)(2,1)S(1)}, bf16[1024,255]{1,0:T(8,128)(2,1)}, u32[]{:S(2)}) copy-start(bf16[1024,255]{1,0:T(8,128)(2,1)} %copy-done.13) | copy-start | bytes 1566724
  114.2 19.6 %collective-permute-start = (bf16[127,4096]{1,0:T(8,128)(2,1)S(1)}, bf16[127,4096]{1,0:T(8,128)(2,1)S(1)}, u32[]{:S(2)}, u32[]{:S(2)}) collective-permute-start(bf16[127,4096]{1,0:T(8,128)(2,1)S(1)} %slice.248), channel_id=1, source_target_pairs={{0,1},{1,2},{2,3},{3,4},{4,5},{5,6},{6,7},{7,8},{8,9},{9,10},{10,1... | collective-permute-start | bytes 3121160 | tf_op jit(solution)/shard_map/ppermute | solution.py:16
  136.8 3.2 copy-start.1
  140.2 10.5 %copy-start.12 = (bf16[1024,255]{1,0:T(8,128)(2,1)S(1)}, bf16[1024,255]{1,0:T(8,128)(2,1)}, u32[]{:S(2)}) copy-start(bf16[1024,255]{1,0:T(8,128)(2,1)} %copy-done.11) | copy-start | bytes 1566724
  152.0 3.2 copy-start.2
  166.1 3.2 copy-start.3
  169.5 9.3 %copy-start.15 = (bf16[1024,255]{0,1:T(8,128)(2,1)S(1)}, bf16[1024,255]{0,1:T(8,128)(2,1)}, u32[]{:S(2)}) copy-start(bf16[1024,255]{0,1:T(8,128)(2,1)} %get-tuple-element.43) | copy-start | bytes 1566724
  180.3 3.2 copy-start.4
  347.5 7.1 %copy-start.7 = (bf16[64,128,255]{2,1,0:T(8,128)(2,1)S(1)}, bf16[64,128,255]{2,1,0:T(8,128)(2,1)}, u32[]{:S(2)}) copy-start(bf16[64,128,255]{2,1,0:T(8,128)(2,1)} %reshape.129) | copy-start | bytes 12533764
  351.0 4.8 %copy-start.9 = (bf16[64,128,255]{2,1,0:T(8,128)(2,1)S(1)}, bf16[64,128,255]{2,1,0:T(8,128)(2,1)}, u32[]{:S(2)}) copy-start(bf16[64,128,255]{2,1,0:T(8,128)(2,1)} %reshape.128) | copy-start | bytes 12533764
  357.0 3.5 copy-start.10
  420.4 1.1 copy-start.16
Sparse Core Ops, SparseCore 0:
  263.2 79.0 all-gather.2
